TPU v7x, 256 devices: a whole 4x4x8 slice. The times are simulated.
256 devices in a mesh: leaf: 64 (over z, x, core), level: 4 (over y).
Axes of the slice: x: 4, y: 4, z: 8, core: 2. Of those that a mesh axis runs over, the one named last changes fastest.
Arguments:
- charges: bfloat16 [3072, 128, 256], P(('leaf', 'level')), may hold values from -6 to 6
- near_mat: bfloat16 [3072, 16, 128, 128], P(('leaf', 'level')), may hold values from -0.1875 to 0.1875
- near_source: int32 [3072, 16], P(('leaf', 'level')), may hold values from 0 to 143
- near_count: int32 [3072], P(('leaf', 'level')), may hold values from 1 to 16, as said below
- moment_map: bfloat16 [3072, 256, 128], P(('leaf', 'level')), may hold values from -0.078125 to 0.078125
- local_eval: bfloat16 [3072, 128, 256], P(('leaf', 'level')), may hold values from -0.375 to 0.375
- upward_child_translation: bfloat16 [8, 256, 256], replicated, may hold values from -0.125 to 0.125
- shift_down: bfloat16 [8, 256, 256], replicated, may hold values from -0.375 to 0.375
- transfer_ops: bfloat16 [8, 256, 256], replicated, may hold values from -0.0625 to 0.0625
- subtree_interaction_list: int32 [64, 32], P('leaf'), may hold values from 0 to 63
- subtree_interaction_operators: int32 [64, 32], P('leaf'), may hold values from 0 to 7
- parent_list: int32 [64, 8], P('leaf'), may hold values from 0 to 7
- parent_ops: int32 [64, 8], P('leaf'), may hold values from 0 to 7
Outputs:
- potential: float32 [3072, 128, 256], P(('leaf', 'level'))
Inputs may be any that keep to these rules, and one draw needn't show every extreme that they name: `near_count`: some block uses all 16 slots and some block only one.
All inputs are finite; a program needn't handle non-finite values.
Results may differ from a plain program's by a relative error of at most 0.012.
Values may be sent and summed in bfloat16 or wider, within the bound.
No kernel may reach another device: no remote copies, remote signals or barrier semaphores. Data moves between devices by JAX's collectives and lax.ppermute only.
A program may use at most 128 MiB of HBM per device.

v0:
```python
import jax
import jax.numpy as jnp
from jax import lax
from jax.sharding import PartitionSpec as P


def extended_2(cells, sides, width):
    for axis, dim in sides:
        count = lax.axis_size(axis)
        ends = count - 1
        head = lax.slice_in_dim(cells, 0, width, axis=dim)
        tail = lax.slice_in_dim(cells, cells.shape[dim] - width, cells.shape[dim], axis=dim)
        cells = jnp.concatenate(
            [
                lax.ppermute(tail, axis, [(i, (i + 1) % count) for i in range(ends)]),
                cells,
                lax.ppermute(head, axis, [((i + 1) % count, i) for i in range(ends)]),
            ],
            axis=dim,
        )
    return cells


def top_tree(
    every,
    upward_child_translation,
    shift_down,
    transfer_ops,
    subtree_interaction_list,
    subtree_interaction_operators,
    parent_list,
    parent_ops,
    leaf_index,
):
    leaves, coeffs, columns = every.shape
    grouped_terms = every.reshape(leaves // 8, 8, coeffs, columns)
    upper_levels = jnp.einsum(
        "get,kgtv->kev", upward_child_translation, grouped_terms, preferred_element_type=jnp.float32
    ).astype(jnp.bfloat16)
    coarse = jnp.einsum(
        "kcd,kdr->cr",
        transfer_ops[parent_ops[0]],
        upper_levels[parent_list[0]],
        preferred_element_type=jnp.float32,
    ).astype(jnp.bfloat16)
    far_leaf = jnp.einsum(
        "kcd,kdr->cr",
        transfer_ops[subtree_interaction_operators[0]],
        every[subtree_interaction_list[0]],
        preferred_element_type=jnp.float32,
    )
    downward = jnp.dot(shift_down[leaf_index % 8], coarse, preferred_element_type=jnp.float32)
    return (far_leaf + downward).astype(jnp.bfloat16)


def on_device(
    charges,
    near_mat,
    near_source,
    near_count,
    moment_map,
    local_eval,
    upward_child_translation,
    shift_down,
    transfer_ops,
    subtree_interaction_list,
    subtree_interaction_operators,
    parent_list,
    parent_ops,
):
    slots = near_mat.shape[1]
    subtree = lax.all_gather(charges, "level", axis=0, tiled=True)
    extended = extended_2(subtree, (("leaf", 0),), subtree.shape[0])
    picked = extended[near_source]
    active = (jnp.arange(slots, dtype=jnp.int32)[None, :] < near_count[:, None]).astype(
        jnp.bfloat16
    )
    picked = picked * active[:, :, None, None]
    near_part = jnp.einsum("bkpq,bkqr->bpr", near_mat, picked, preferred_element_type=jnp.float32)
    partial_moment = jnp.einsum(
        "bcp,bpr->cr", moment_map, charges, preferred_element_type=jnp.float32
    )
    leaf_index = lax.axis_index("leaf")
    moment = lax.psum(partial_moment.astype(jnp.bfloat16), "level")
    every = lax.all_gather(moment[None], "leaf", axis=0, tiled=True)
    local_part = top_tree(
        every,
        upward_child_translation,
        shift_down,
        transfer_ops,
        subtree_interaction_list,
        subtree_interaction_operators,
        parent_list,
        parent_ops,
        leaf_index,
    )
    far_part = jnp.einsum("bpc,cr->bpr", local_eval, local_part, preferred_element_type=jnp.float32)
    return near_part + far_part


def solution(mesh):
    placed = (
        P(("leaf", "level"), None, None),
        P(("leaf", "level"), None, None, None),
        P(("leaf", "level"), None),
        P(("leaf", "level")),
        P(("leaf", "level"), None, None),
        P(("leaf", "level"), None, None),
        P(),
        P(),
        P(),
        P("leaf", None),
        P("leaf", None),
        P("leaf", None),
        P("leaf", None),
    )
    return jax.shard_map(
        on_device,
        mesh=mesh,
        in_specs=placed,
        out_specs=P(("leaf", "level"), None, None),
        check_vma=False,
    )
```

profile of v0, /device:TPU:103, one launch (start us, length us, event | category | flops | bytes accessed | tf_op | source)
XLA Modules:
  0.0 231.8 jit_solution(3247410838116859868)
XLA Ops:
  6.5 2.5 %fusion.10 = bf16[1,256,256]{2,1,0:T(8,128)(2,1)} fusion(bf16[12,256,128]{2,1,0:T(8,128)(2,1)} %param.17, bf16[12,128,256]{2,1,0:T(8,128)(2,1)} %param.13), kind=kOutput, calls=%fused_computation.20 | convolution fusion | flops 201392128 | bytes 1703936 | tf_op jit(solution)/shard_map/bcp,bpr->cr/dot_general | solution.py:80
  9.1 0.7 all-gather.3.cloned.1.call-update
  9.8 46.2 %all-reduce.2.cloned.1.call-done = bf16[1,256,256]{2,1,0:T(8,128)(2,1)} async-done(((bf16[1,256,256]{2,1,0:T(8,128)(2,1)}), bf16[1,256,256]{2,1,0:T(8,128)(2,1)}) %all-reduce.2.cloned.1.call-update) | async-done | bytes 131088 | tf_op jit(solution)/shard_map/psum | solution.py:84
  56.0 46.2 %all-gather.3.cloned.1.call-done = bf16[48,128,256]{2,1,0:T(8,128)(2,1)} async-done(((bf16[12,128,256]{2,1,0:T(8,128)(2,1)}), bf16[48,128,256]{2,1,0:T(8,128)(2,1)}) %all-gather.3.cloned.1.call-update) | async-done | bytes 3145744 | tf_op jit(solution)/shard_map/all_gather | solution.py:72
  102.2 5.1 %collective-permute-start = (bf16[48,128,256]{2,1,0:T(8,128)(2,1)}, bf16[48,128,256]{2,1,0:T(8,128)(2,1)}, u32[]{:S(2)}, u32[]{:S(2)}) collective-permute-start(bf16[48,128,256]{2,1,0:T(8,128)(2,1)} %all-gather.3.cloned.1.call-done), channel_id=1, source_target_pairs={{0,4},{4,8},{8,12},{12,16},{16,20},{20,24},{24,28},{28,32},{32,36}... | collective-permute-start | bytes 9437192 | tf_op jit(solution)/shard_map/ppermute | solution.py:15
  107.3 1.9 collective-permute-start.1
  109.3 0.7 fusion.15
  110.0 2.9 %gather_fusion.1 = bf16[32,256,256]{2,1,0:T(8,128)(2,1)} fusion(bf16[8,256,256]{2,1,0:T(8,128)(2,1)S(1)} %copy-done, s32[1024]{0:T(1024)S(1)} %pad_clamp_fusion.3), kind=kCustom, calls=%fused_computation.1 | custom fusion | bytes 8388736 | tf_op jit(solution)/shard_map/gather | solution.py:48
  112.9 0.6 gather_fusion.3
  113.6 0.1 reshape.140
  113.8 33.0 %collective-permute-done = bf16[48,128,256]{2,1,0:T(8,128)(2,1)} collective-permute-done((bf16[48,128,256]{2,1,0:T(8,128)(2,1)}, bf16[48,128,256]{2,1,0:T(8,128)(2,1)}, u32[]{:S(2)}, u32[]{:S(2)}) %collective-permute-start) | collective-permute-done | bytes 3145760 | tf_op jit(solution)/shard_map/ppermute | solution.py:15
  146.8 7.7 %collective-permute-done.1 = bf16[48,128,256]{2,1,0:T(8,128)(2,1)} collective-permute-done((bf16[48,128,256]{2,1,0:T(8,128)(2,1)}, bf16[48,128,256]{2,1,0:T(8,128)(2,1)}, u32[]{:S(2)}, u32[]{:S(2)}) %collective-permute-start.1) | collective-permute-done | bytes 3145760 | tf_op jit(solution)/shard_map/ppermute | solution.py:17
  154.5 8.4 %pad_maximum_fusion = bf16[144,128,256]{2,1,0:T(8,128)(2,1)} fusion(bf16[48,128,256]{2,1,0:T(8,128)(2,1)} %collective-permute-done.1, bf16[48,128,256]{2,1,0:T(8,128)(2,1)} %all-gather.3.cloned.1.call-done, bf16[48,128,256]{2,1,0:T(8,128)(2,1)} %collective-permute-done), kind=kLoop, calls=%fused_computation.7 | loop fusion | flops 9437184 | bytes 18874368 | tf_op jit(solution)/shard_map/concatenate | solution.py:13
  162.9 12.0 %gather_fusion = bf16[192,128,256]{2,1,0:T(8,128)(2,1)} fusion(bf16[144,128,256]{2,1,0:T(8,128)(2,1)} %pad_maximum_fusion, s32[1024]{0:T(1024)S(1)} %pad_clamp_fusion.4), kind=kCustom, calls=%fused_computation | custom fusion | bytes 25166592 | tf_op jit(solution)/shard_map/gather | solution.py:74
  174.9 16.8 %copy.16 = bf16[12,16,128,256]{2,3,1,0:T(8,128)(2,1)} copy(bf16[12,16,128,256]{3,2,1,0:T(8,128)(2,1)} %bitcast.66) | data formatting | bytes 25165824 | tf_op jit(solution)/shard_map/gather | solution.py:74
  191.6 6.1 %gather_fusion.2 = bf16[32,256,256]{2,1,0:T(8,128)(2,1)} fusion(bf16[64,256,256]{2,1,0:T(8,128)(2,1)} %all-gather.5.cloned.1.call-done, s32[1024]{0:T(1024)S(1)} %pad_clamp_fusion.2), kind=kCustom, calls=%fused_computation.2 | custom fusion | bytes 8388736 | tf_op jit(solution)/shard_map/gather | solution.py:49
  197.8 5.3 %convolution_bitcast_fusion.1 = f32[256,256]{0,1:T(8,128)S(1)} fusion(bf16[32,256,256]{2,1,0:T(8,128)(2,1)} %gather_fusion.1, bf16[32,256,256]{2,1,0:T(8,128)(2,1)} %gather_fusion.2), kind=kOutput, calls=%fused_computation.14 | convolution fusion | flops 1073741824 | bytes 8650752 | tf_op jit(solution)/shard_map/kcd,kdr->cr/dot_general | solution.py:46
  203.1 0.5 copy-done.2
  203.6 3.7 %fusion.5 = bf16[8,256,256]{1,2,0:T(8,128)(2,1)S(1)} fusion(bf16[8,8,256,256]{3,2,1,0:T(8,128)(2,1)S(1)} %bitcast.67, bf16[8,256,256]{2,1,0:T(8,128)(2,1)} %param.19), kind=kOutput, calls=%fused_computation.11 | convolution fusion | flops 2148007936 | bytes 10485760 | tf_op jit(solution)/shard_map/get,kgtv->kev/dot_general | solution.py:37
  207.3 0.6 gather_fusion.4
  207.9 1.7 fusion.9
  209.6 1.5 fusion.20
  211.2 11.1 %bitcast_add_fusion = f32[12,128,256]{1,2,0:T(8,128)} fusion(f32[256,12,128]{2,0,1:T(8,128)S(1)} %fusion.20, bf16[12,16,128,128]{3,2,1,0:T(8,128)(2,1)} %param.14, bf16[12,16,128,256]{2,3,1,0:T(8,128)(2,1)} %copy.16, bf16[12,16]{1,0:T(8,128)(2,1)S(1)} %fusion.14), kind=kOutput, calls=%fused_computation.10 | convolution fusion | flops 1617297408 | bytes 22020480 | tf_op jit(solution)/shard_map/bkpq,bkqr->bpr/dot_general | solution.py:79
  222.3 3.0 %copy.17 = f32[12,128,256]{2,1,0:T(8,128)} copy(f32[12,128,256]{1,2,0:T(8,128)} %bitcast_add_fusion) | data formatting | bytes 3145728 | tf_op jit(solution)/shard_map/add | solution.py:98
  (31 shorter events, 0.3 us)
Async XLA Ops:
  6.5 103.4 %copy-start = (bf16[8,256,256]{2,1,0:T(8,128)(2,1)S(1)}, bf16[8,256,256]{2,1,0:T(8,128)(2,1)}, u32[]{:S(2)}) copy-start(bf16[8,256,256]{2,1,0:T(8,128)(2,1)} %param.21) | copy-start | bytes 3145732
  6.5 49.5 %all-reduce.2.cloned.1.call-start = ((), (), s32[]{:S(2)}) async-start(), calls=%async_computation.1 | async-start | bytes 262144 | tf_op jit(solution)/shard_map/psum | solution.py:84
  9.1 93.2 %all-gather.3.cloned.1.call-start = ((), (), s32[]{:S(2)}) async-start(), calls=%async_computation | async-start | bytes 3932160 | tf_op jit(solution)/shard_map/all_gather | solution.py:72
  9.8 181.8 %all-gather.5.cloned.1.call-start = ((), (), s32[]{:S(2)}) async-start(), calls=%async_computation.2 | async-start | bytes 8519680 | tf_op jit(solution)/shard_map/all_gather | solution.py:85
  102.2 44.5 %collective-permute-start = (bf16[48,128,256]{2,1,0:T(8,128)(2,1)}, bf16[48,128,256]{2,1,0:T(8,128)(2,1)}, u32[]{:S(2)}, u32[]{:S(2)}) collective-permute-start(bf16[48,128,256]{2,1,0:T(8,128)(2,1)} %all-gather.3.cloned.1.call-done), channel_id=1, source_target_pairs={{0,4},{4,8},{8,12},{12,16},{16,20},{20,24},{24,28},{28,32},{32,36}... | collective-permute-start | bytes 9437192 | tf_op jit(solution)/shard_map/ppermute | solution.py:15
  107.3 47.1 %collective-permute-start.1 = (bf16[48,128,256]{2,1,0:T(8,128)(2,1)}, bf16[48,128,256]{2,1,0:T(8,128)(2,1)}, u32[]{:S(2)}, u32[]{:S(2)}) collective-permute-start(bf16[48,128,256]{2,1,0:T(8,128)(2,1)} %all-gather.3.cloned.1.call-done), channel_id=1, source_target_pairs={{4,0},{8,4},{12,8},{16,12},{20,16},{24,20},{28,24},{32,28},{36,32}... | collective-permute-start | bytes 9437192 | tf_op jit(solution)/shard_map/ppermute | solution.py:17
  110.0 2.9 %copy-start.5 = (s32[1,8]{1,0:T(1,128)S(1)}, s32[1,8]{1,0:T(1,128)}, u32[]{:S(2)}) copy-start(s32[1,8]{1,0:T(1,128)} %param.25) | copy-start | bytes 100
  110.0 3.6 %copy-start.3 = (s32[12,16]{1,0:T(8,128)S(1)}, s32[12,16]{1,0:T(8,128)}, u32[]{:S(2)}) copy-start(s32[12,16]{1,0:T(8,128)} %param.15) | copy-start | bytes 2308
  110.0 3.6 %copy-start.6 = (s32[1,32]{1,0:T(1,128)S(1)}, s32[1,32]{1,0:T(1,128)}, u32[]{:S(2)}) copy-start(s32[1,32]{1,0:T(1,128)} %param.22) | copy-start | bytes 388
  110.0 3.7 %copy-start.7 = (s32[1,8]{1,0:T(1,128)S(1)}, s32[1,8]{1,0:T(1,128)}, u32[]{:S(2)}) copy-start(s32[1,8]{1,0:T(1,128)} %param.24) | copy-start | bytes 100
  110.0 3.7 %copy-start.4 = (s32[12]{0:T(128)S(1)}, s32[12]{0:T(128)}, u32[]{:S(2)}) copy-start(s32[12]{0:T(128)} %param.16) | copy-start | bytes 148
  197.8 5.8 %copy-start.2 = (bf16[64,256,256]{2,1,0:T(8,128)(2,1)S(1)}, bf16[64,256,256]{2,1,0:T(8,128)(2,1)}, u32[]{:S(2)}) copy-start(bf16[64,256,256]{2,1,0:T(8,128)(2,1)} %all-gather.5.cloned.1.call-done) | copy-start | bytes 25165828
  211.1 14.2 %copy-start.1 = (bf16[8,256,256]{2,1,0:T(8,128)(2,1)S(1)}, bf16[8,256,256]{2,1,0:T(8,128)(2,1)}, u32[]{:S(2)}) copy-start(bf16[8,256,256]{2,1,0:T(8,128)(2,1)} %param.21) | copy-start | bytes 3145732
Sparse Core Ops, SparseCore 0:
  9.6 46.3 all-reduce.1
  57.8 44.3 all-gather.2
  105.0 81.0 all-gather.4
where the time goes:
time: 233 us; the launch traced here: 232 us
  waiting for transfers between devices  134 us (58%)
  local copies, waits for them, and re-layouts  42.6 us (18%)
  matrix products  25.9 us (11%)
  between operations  13.3 us (6%)
  other arithmetic  9.2 us (4%)
  starting transfers between devices  7.09 us (3%)
    all_gather x1, waiting for transfers between devices, on_device(): subtree = lax.all_gather(charges, 'level', axis=0, tiled=True)  46.2 us
    psum x1, waiting for transfers between devices, on_device(): moment = lax.psum(partial_moment.astype(jnp.bfloat16), 'level')  46.2 us
    ppermute x1, waiting for transfers between devices, extended_2(): lax.ppermute(tail, axis, [(i, (i + 1) % count) for i in range(ends)])  33 us
    gather x2, local copies, waits for them, and re-layouts, on_device(): picked = extended[near_source]  28.7 us
    dot_general x1, matrix products, on_device(): jnp.einsum('bkpq,bkqr->bpr', near_mat, picked, preferred_element_type=jnp...  11.1 us
    concatenate x1, other arithmetic, extended_2(): jnp.concatenate([lax.ppermute(tail, axis, [(i, (i + 1) % count) for i in...  8.42 us
    ppermute x1, waiting for transfers between devices, extended_2(): lax.ppermute(head, axis, [((i + 1) % count, i) for i in range(ends)])  7.72 us
    gather x1, local copies, waits for them, and re-layouts, top_tree(): every[subtree_interaction_list[0]]  6.13 us
  transfers between devices with their start and end apart: 5, of which 4 were waited for; matrix products, arithmetic and copies ran while one was open for 18% of the time, Pallas kernels for 0%

commit v1 on v0

--- a/solution.py
+++ b/solution.py
@@ -69,7 +69,13 @@
     parent_ops,
 ):
     slots = near_mat.shape[1]
-    subtree = lax.all_gather(charges, "level", axis=0, tiled=True)
+    r_now = lax.all_to_all(
+        jnp.stack([charges for _ in range(lax.psum(1, "level"))]),
+        axis_name="level",
+        split_axis=0,
+        concat_axis=0,
+    )
+    subtree = jnp.concatenate(r_now, 0)
     extended = extended_2(subtree, (("leaf", 0),), subtree.shape[0])
     picked = extended[near_source]
     active = (jnp.arange(slots, dtype=jnp.int32)[None, :] < near_count[:, None]).astype(

time: 233 us -> 241 us (1.034)
  blocking collectives: 0 us -> 38 us
  waiting for transfers between devices: 134 us -> 102 us
  starting transfers between devices: 7.09 us -> 10.1 us
    all_gather x1 -> x0, waiting for transfers between devices: 46.2 us -> none  [on_device(): subtree = lax.all_gather(charges, 'level', axis=0, tiled=True)]
    all_to_all x0 -> x1, blocking collectives: none -> 38 us  [on_device(): lax.all_to_all(jnp.stack([charges for _ in range(lax.psum(1, 'level'))]),...]
    ppermute x1, waiting for transfers between devices: 33 us -> 44.1 us  [extended_2(): lax.ppermute(tail, axis, [(i, (i + 1) % count) for i in range(ends)])]
    ppermute x1, starting transfers between devices: 5.09 us -> 8.14 us  [extended_2(): lax.ppermute(tail, axis, [(i, (i + 1) % count) for i in range(ends)])]
    ppermute x1, waiting for transfers between devices: 7.72 us -> 10.7 us  [extended_2(): lax.ppermute(head, axis, [((i + 1) % count, i) for i in range(ends)])]
  transfers between devices with their start and end apart: 5 -> 4, of which waited for: 4 -> 3; matrix products, arithmetic and copies ran while one was open for 18% -> 17% of each run, Pallas kernels for 0% -> 0%
where the time goes in v1:
time: 241 us; the launch traced here: 240 us
  waiting for transfers between devices  102 us (42%)
  local copies, waits for them, and re-layouts  44.6 us (19%)
  blocking collectives  38 us (16%)
  matrix products  24 us (10%)
  between operations  13.6 us (6%)
  starting transfers between devices  10.1 us (4%)
  other arithmetic  7.96 us (3%)
    psum x1, waiting for transfers between devices, on_device(): moment = lax.psum(partial_moment.astype(jnp.bfloat16), 'level')  46.9 us
    ppermute x1, waiting for transfers between devices, extended_2(): lax.ppermute(tail, axis, [(i, (i + 1) % count) for i in range(ends)])  44.1 us
    all_to_all x1, blocking collectives, on_device(): lax.all_to_all(jnp.stack([charges for _ in range(lax.psum(1, 'level'))]),...  38 us
    gather x2, local copies, waits for them, and re-layouts, on_device(): picked = extended[near_source]  28.5 us
    dot_general x1, matrix products, on_device(): jnp.einsum('bkpq,bkqr->bpr', near_mat, picked, preferred_element_type=jnp...  11.1 us
    ppermute x1, waiting for transfers between devices, extended_2(): lax.ppermute(head, axis, [((i + 1) % count, i) for i in range(ends)])  10.7 us
    ppermute x1, starting transfers between devices, extended_2(): lax.ppermute(tail, axis, [(i, (i + 1) % count) for i in range(ends)])  8.14 us
    concatenate x1, other arithmetic, extended_2(): jnp.concatenate([lax.ppermute(tail, axis, [(i, (i + 1) % count) for i in...  7.84 us
  transfers between devices with their start and end apart: 4, of which 3 were waited for; matrix products, arithmetic and copies ran while one was open for 17% of the time, Pallas kernels for 0%

profile of v1, /device:TPU:103, one launch (start us, length us, event | category | flops | bytes accessed | tf_op | source)
XLA Modules:
  0.0 240.1 jit_solution(6402833683073933182)
XLA Ops:
  6.5 2.5 %fusion.10 = bf16[1,256,256]{2,1,0:T(8,128)(2,1)} fusion(bf16[12,256,128]{2,1,0:T(8,128)(2,1)} %param.17, bf16[12,128,256]{2,1,0:T(8,128)(2,1)} %param.13), kind=kOutput, calls=%fused_computation.20 | convolution fusion | flops 201392128 | bytes 1703936 | tf_op jit(solution)/shard_map/bcp,bpr->cr/dot_general | solution.py:86
  9.1 46.9 %all-reduce.2.cloned.1.call-done = bf16[1,256,256]{2,1,0:T(8,128)(2,1)} async-done(((bf16[1,256,256]{2,1,0:T(8,128)(2,1)}), bf16[1,256,256]{2,1,0:T(8,128)(2,1)}) %all-reduce.2.cloned.1.call-update) | async-done | bytes 131088 | tf_op jit(solution)/shard_map/psum | solution.py:90
  56.0 1.5 stack.2
  57.5 38.0 %all_to_all.5 = bf16[4,12,128,256]{3,2,1,0:T(8,128)(2,1)} all-to-all(bf16[4,12,128,256]{3,2,1,0:T(8,128)(2,1)S(1)} %stack.2), channel_id=1, replica_groups=mesh['leaf'=64,'level'=4] {'level'}, dimensions={0} | all-to-all | bytes 6291456 | tf_op jit(solution)/shard_map/all_to_all | solution.py:72
  95.5 8.1 %collective-permute-start = (bf16[48,128,256]{2,1,0:T(8,128)(2,1)}, bf16[48,128,256]{2,1,0:T(8,128)(2,1)}, u32[]{:S(2)}, u32[]{:S(2)}) collective-permute-start(bf16[48,128,256]{2,1,0:T(8,128)(2,1)} %bitcast), channel_id=1, source_target_pairs={{0,4},{4,8},{8,12},{12,16},{16,20},{20,24},{24,28},{28,32},{32,36}... | collective-permute-start | bytes 9437192 | tf_op jit(solution)/shard_map/ppermute | solution.py:15
  103.7 1.9 collective-permute-start.1
  105.7 2.9 %gather_fusion.1 = bf16[32,256,256]{2,1,0:T(8,128)(2,1)} fusion(bf16[8,256,256]{2,1,0:T(8,128)(2,1)S(1)} %copy-done, s32[1024]{0:T(1024)S(1)} %pad_clamp_fusion.3), kind=kCustom, calls=%fused_computation.1 | custom fusion | bytes 8388736 | tf_op jit(solution)/shard_map/gather | solution.py:48
  108.6 0.6 gather_fusion.3
  109.3 0.1 reshape.146
  109.5 44.1 %collective-permute-done = bf16[48,128,256]{2,1,0:T(8,128)(2,1)} collective-permute-done((bf16[48,128,256]{2,1,0:T(8,128)(2,1)}, bf16[48,128,256]{2,1,0:T(8,128)(2,1)}, u32[]{:S(2)}, u32[]{:S(2)}) %collective-permute-start) | collective-permute-done | bytes 3145760 | tf_op jit(solution)/shard_map/ppermute | solution.py:15
  153.6 10.7 %collective-permute-done.1 = bf16[48,128,256]{2,1,0:T(8,128)(2,1)} collective-permute-done((bf16[48,128,256]{2,1,0:T(8,128)(2,1)}, bf16[48,128,256]{2,1,0:T(8,128)(2,1)}, u32[]{:S(2)}, u32[]{:S(2)}) %collective-permute-start.1) | collective-permute-done | bytes 3145760 | tf_op jit(solution)/shard_map/ppermute | solution.py:17
  164.3 7.8 %pad_maximum_fusion = bf16[144,128,256]{2,1,0:T(8,128)(2,1)} fusion(bf16[48,128,256]{2,1,0:T(8,128)(2,1)} %collective-permute-done.1, bf16[48,128,256]{2,1,0:T(8,128)(2,1)} %bitcast, bf16[48,128,256]{2,1,0:T(8,128)(2,1)} %collective-permute-done), kind=kLoop, calls=%fused_computation.7 | loop fusion | flops 9437184 | bytes 18874368 | tf_op jit(solution)/shard_map/concatenate | solution.py:13
  172.2 11.8 %gather_fusion = bf16[192,128,256]{2,1,0:T(8,128)(2,1)} fusion(bf16[144,128,256]{2,1,0:T(8,128)(2,1)} %pad_maximum_fusion, s32[1024]{0:T(1024)S(1)} %pad_clamp_fusion.4), kind=kCustom, calls=%fused_computation | custom fusion | bytes 25166592 | tf_op jit(solution)/shard_map/gather | solution.py:80
  184.0 16.7 %copy.17 = bf16[12,16,128,256]{2,3,1,0:T(8,128)(2,1)} copy(bf16[12,16,128,256]{3,2,1,0:T(8,128)(2,1)} %bitcast.68) | data formatting | bytes 25165824 | tf_op jit(solution)/shard_map/gather | solution.py:80
  200.7 6.1 %gather_fusion.2 = bf16[32,256,256]{2,1,0:T(8,128)(2,1)} fusion(bf16[64,256,256]{2,1,0:T(8,128)(2,1)} %all-gather.2.cloned.1.call-done, s32[1024]{0:T(1024)S(1)} %pad_clamp_fusion.2), kind=kCustom, calls=%fused_computation.2 | custom fusion | bytes 8388736 | tf_op jit(solution)/shard_map/gather | solution.py:49
  206.8 4.8 %convolution_bitcast_fusion.1 = f32[256,256]{1,0:T(8,128)S(1)} fusion(bf16[32,256,256]{2,1,0:T(8,128)(2,1)} %gather_fusion.1, bf16[32,256,256]{2,1,0:T(8,128)(2,1)} %gather_fusion.2), kind=kOutput, calls=%fused_computation.14 | convolution fusion | flops 1073741824 | bytes 8650752 | tf_op jit(solution)/shard_map/kcd,kdr->cr/dot_general | solution.py:46
  211.7 1.0 copy-done.2
  212.7 0.2 copy-done.5
  212.9 2.4 fusion.5
  215.3 0.6 gather_fusion.4
  215.9 1.6 fusion.9
  217.5 1.6 fusion.20
  219.1 11.1 %bitcast_add_fusion = f32[12,128,256]{1,2,0:T(8,128)} fusion(f32[256,12,128]{2,0,1:T(8,128)S(1)} %fusion.20, bf16[12,16,128,128]{3,2,1,0:T(8,128)(2,1)} %param.14, bf16[12,16,128,256]{2,3,1,0:T(8,128)(2,1)} %copy.17, bf16[12,16]{1,0:T(8,128)(2,1)S(1)} %fusion.14), kind=kOutput, calls=%fused_computation.10 | convolution fusion | flops 1617297408 | bytes 22020480 | tf_op jit(solution)/shard_map/bkpq,bkqr->bpr/dot_general | solution.py:85
  230.2 3.0 %copy.21 = f32[12,128,256]{2,1,0:T(8,128)} copy(f32[12,128,256]{1,2,0:T(8,128)} %bitcast_add_fusion) | data formatting | bytes 3145728 | tf_op jit(solution)/shard_map/add | solution.py:104
  (34 shorter events, 0.3 us)
Async XLA Ops:
  6.5 99.1 %copy-start = (bf16[8,256,256]{2,1,0:T(8,128)(2,1)S(1)}, bf16[8,256,256]{2,1,0:T(8,128)(2,1)}, u32[]{:S(2)}) copy-start(bf16[8,256,256]{2,1,0:T(8,128)(2,1)} %param.21) | copy-start | bytes 3145732
  6.5 49.5 %all-reduce.2.cloned.1.call-start = ((), (), s32[]{:S(2)}) async-start(), calls=%async_computation.1 | async-start | bytes 262144 | tf_op jit(solution)/shard_map/psum | solution.py:90
  9.1 191.7 %all-gather.2.cloned.1.call-start = ((), (), s32[]{:S(2)}) async-start(), calls=%async_computation.2 | async-start | bytes 8519680 | tf_op jit(solution)/shard_map/all_gather | solution.py:91
  56.0 49.6 %copy-start.6 = (s32[1,32]{1,0:T(1,128)S(1)}, s32[1,32]{1,0:T(1,128)}, u32[]{:S(2)}) copy-start(s32[1,32]{1,0:T(1,128)} %param.23) | copy-start | bytes 388
  95.5 58.1 %collective-permute-start = (bf16[48,128,256]{2,1,0:T(8,128)(2,1)}, bf16[48,128,256]{2,1,0:T(8,128)(2,1)}, u32[]{:S(2)}, u32[]{:S(2)}) collective-permute-start(bf16[48,128,256]{2,1,0:T(8,128)(2,1)} %bitcast), channel_id=1, source_target_pairs={{0,4},{4,8},{8,12},{12,16},{16,20},{20,24},{24,28},{28,32},{32,36}... | collective-permute-start | bytes 9437192 | tf_op jit(solution)/shard_map/ppermute | solution.py:15
  103.7 60.7 %collective-permute-start.1 = (bf16[48,128,256]{2,1,0:T(8,128)(2,1)}, bf16[48,128,256]{2,1,0:T(8,128)(2,1)}, u32[]{:S(2)}, u32[]{:S(2)}) collective-permute-start(bf16[48,128,256]{2,1,0:T(8,128)(2,1)} %bitcast), channel_id=1, source_target_pairs={{4,0},{8,4},{12,8},{16,12},{20,16},{24,20},{28,24},{32,28},{36,32}... | collective-permute-start | bytes 9437192 | tf_op jit(solution)/shard_map/ppermute | solution.py:17
  105.7 2.9 %copy-start.7 = (s32[1,8]{1,0:T(1,128)S(1)}, s32[1,8]{1,0:T(1,128)}, u32[]{:S(2)}) copy-start(s32[1,8]{1,0:T(1,128)} %param.25) | copy-start | bytes 100
  105.7 3.6 %copy-start.3 = (s32[12,16]{1,0:T(8,128)S(1)}, s32[12,16]{1,0:T(8,128)}, u32[]{:S(2)}) copy-start(s32[12,16]{1,0:T(8,128)} %param.15) | copy-start | bytes 2308
  105.7 3.6 %copy-start.8 = (s32[1,32]{1,0:T(1,128)S(1)}, s32[1,32]{1,0:T(1,128)}, u32[]{:S(2)}) copy-start(s32[1,32]{1,0:T(1,128)} %param.22) | copy-start | bytes 388
  105.7 3.7 %copy-start.9 = (s32[1,8]{1,0:T(1,128)S(1)}, s32[1,8]{1,0:T(1,128)}, u32[]{:S(2)}) copy-start(s32[1,8]{1,0:T(1,128)} %param.24) | copy-start | bytes 100
  105.7 3.7 %copy-start.4 = (s32[12]{0:T(128)S(1)}, s32[12]{0:T(128)}, u32[]{:S(2)}) copy-start(s32[12]{0:T(128)} %param.16) | copy-start | bytes 148
  206.8 5.8 %copy-start.2 = (bf16[64,256,256]{2,1,0:T(8,128)(2,1)S(1)}, bf16[64,256,256]{2,1,0:T(8,128)(2,1)}, u32[]{:S(2)}) copy-start(bf16[64,256,256]{2,1,0:T(8,128)(2,1)} %all-gather.2.cloned.1.call-done) | copy-start | bytes 25165828
  206.8 6.1 %copy-start.5 = (bf16[8,256,256]{2,1,0:T(8,128)(2,1)S(1)}, bf16[8,256,256]{2,1,0:T(8,128)(2,1)}, u32[]{:S(2)}) copy-start(bf16[8,256,256]{2,1,0:T(8,128)(2,1)} %param.19) | copy-start | bytes 3145732
  219.1 14.2 %copy-start.1 = (bf16[8,256,256]{2,1,0:T(8,128)(2,1)S(1)}, bf16[8,256,256]{2,1,0:T(8,128)(2,1)}, u32[]{:S(2)}) copy-start(bf16[8,256,256]{2,1,0:T(8,128)(2,1)} %param.21) | copy-start | bytes 3145732
Sparse Core Ops, SparseCore 0:
  9.6 46.3 all-reduce.1
  58.8 108.4 all-gather.1
